TPU v7x, 256 devices: a whole 4x4x8 slice. The times are simulated.
256 devices in a mesh: rows: 8 (over x, core), cols: 32 (over y, z).
Axes of the slice: x: 4, y: 4, z: 8, core: 2. Of those that a mesh axis runs over, the one named last changes fastest.
Arguments:
- features: bfloat16 [256, 4096, 1536], P('rows', 'cols'), may hold values from -6 to 6
- projection: bfloat16 [1536, 128], replicated, may hold values from -0.4375 to 0.4375
- prev_dist: float32 [256, 4096], P('rows', 'cols'), may hold values from 0.5 to 3
- valid: int32 [256, 4096], P('rows', 'cols'), may hold values 0 or 1
- pick_owner: int32 [512], replicated, may hold values from 0 to 255, as said below
- pick_slot: int32 [512], replicated, may hold values from 0 to 4095, as said below
Outputs:
- min_dist: float32 [256, 4096], P('rows', 'cols')
Inputs may be any that keep to these rules, and one draw needn't show every extreme that they name: `pick_owner`: no two picks name the same patch; picks fall on devices at random. `pick_slot`: see pick_owner.
All inputs are finite; a program needn't handle non-finite values. No bound on the sum of `valid` on one device may be relied on, other than what follows from the above.
Results may differ from a plain program's by a relative error of at most 0.0003.
Values may be sent and summed in bfloat16 or wider, within the bound.
A program may use at most 128 MiB of HBM per device.

v0:
```python
import jax
import jax.numpy as jnp
from jax import lax
from jax.sharding import PartitionSpec as P

D_PROJ = 128


def padded_2(block, sides, width):
    for axis, dim in sides:
        count = lax.axis_size(axis)
        forward = [(i, i + 1) for i in range(count - 1)]
        backward = [(target, source) for source, target in forward]
        low = lax.ppermute(
            lax.slice_in_dim(block, block.shape[dim] - width, None, axis=dim), axis, forward
        )
        high = lax.ppermute(lax.slice_in_dim(block, 0, width, axis=dim), axis, backward)
        block = jnp.concatenate([low, block, high], axis=dim)
    return block


def window_sum(padded, rows_dev, cols_dev):
    total = jnp.zeros((rows_dev, cols_dev, padded.shape[2]), jnp.float32)
    for row_off in range(3):
        for col_off in range(3):
            total = total + padded[
                row_off : row_off + rows_dev, col_off : col_off + cols_dev
            ].astype(jnp.float32)
    return total / 9.0


def shards(features, projection, prev_dist, valid, pick_owner, pick_slot):
    rows_dev, cols_dev, channels = features.shape
    proj_full = projection.astype(jnp.float32)
    own_index = lax.axis_index("rows") * lax.axis_size("cols") + lax.axis_index("cols")
    owned = pick_owner == own_index
    padded = padded_2(features, (("rows", 0), ("cols", 1)), 1)
    pooled = window_sum(padded, rows_dev, cols_dev).reshape(rows_dev * cols_dev, channels)
    projected = jnp.dot(pooled, proj_full, precision=lax.Precision.HIGHEST)
    local_rows = jnp.where(owned[:, None], projected[pick_slot], jnp.float32(0.0))
    pick_rows = lax.psum(local_rows, ("rows", "cols"))
    pick_sq = jnp.sum(pick_rows * pick_rows, axis=1)
    own_sq = jnp.sum(projected * projected, axis=1)
    inner_prod = jnp.dot(projected, pick_rows.T, precision=lax.Precision.HIGHEST)
    scaled_gap = (own_sq[:, None] + pick_sq[None, :] - 2.0 * inner_prod) / D_PROJ
    nearest = jnp.min(scaled_gap, axis=1).reshape(rows_dev, cols_dev)
    return jnp.where(valid == 1, jnp.minimum(prev_dist, nearest), jnp.float32(0.0))


def solution(mesh):
    return jax.shard_map(
        shards,
        mesh=mesh,
        in_specs=(P("rows", "cols", None), P(), P("rows", "cols"), P("rows", "cols"), P(), P()),
        out_specs=P("rows", "cols"),
        check_vma=False,
    )
```

profile of v0, /device:TPU:2, one launch (start us, length us, event | category | flops | bytes accessed | tf_op | source)
XLA Modules:
  0.0 382.1 jit_solution(17740806826330092399)
XLA Ops:
  6.5 0.0 copy-start
  6.5 0.0 all-reduce.2.cloned.1.call-start
  6.5 1.2 fusion.6
  7.8 1.9 collective-permute-start
  9.7 3.6 collective-permute-start.1
  13.3 0.7 broadcast_compare_fusion
  14.0 0.7 compare_select_fusion
  14.7 2.1 collective-permute-done
  16.9 6.7 %constant_dynamic-update-slice_fusion.1 = bf16[34,128,1536]{2,1,0:T(8,128)(2,1)S(1)} fusion(bf16[34,128,1536]{2,1,0:T(8,128)(2,1)S(1)} %constant_dynamic-update-slice_fusion.2, bf16[32,128,1536]{2,1,0:T(8,128)(2,1)} %param.6), kind=kLoop, calls=%fused_computation.25 | loop fusion | bytes 25165824
  23.6 0.0 collective-permute-done.1
  23.6 0.0 copy-start.1
  23.6 4.8 %copy-done.1 = bf16[34,128,1536]{2,1,0:T(8,128)(2,1)} copy-done((bf16[34,128,1536]{2,1,0:T(8,128)(2,1)}, bf16[34,128,1536]{2,1,0:T(8,128)(2,1)S(1)}, u32[]{:S(2)}) %copy-start.1) | copy-done | bytes 13369368
  28.5 0.3 fusion.5
  28.8 3.8 %collective-permute-start.2 = (bf16[34,1,1536]{2,0,1:T(8,128)(2,1)S(1)}, bf16[34,1,1536]{2,0,1:T(8,128)(2,1)S(1)}, u32[]{:S(2)}, u32[]{:S(2)}) collective-permute-start(bf16[34,1,1536]{2,0,1:T(8,128)(2,1)S(1)} %copy.15), channel_id=1, source_target_pairs={{0,1},{1,2},{2,3},{3,4},{4,5},{5,6},{6,7},{7,8},{8,9},{9,10},{10,1... | collective-permute-start | bytes 313352 | tf_op jit(solution)/shard_map/ppermute | solution.py:14
  32.7 1.3 collective-permute-start.3
  34.0 1.1 collective-permute-done.2
  35.1 0.2 copy.16
  35.2 4.2 %collective-permute-done.3 = bf16[34,1,1536]{2,0,1:T(8,128)(2,1)S(1)} collective-permute-done((bf16[34,1,1536]{2,0,1:T(8,128)(2,1)S(1)}, bf16[34,1,1536]{2,0,1:T(8,128)(2,1)S(1)}, u32[]{:S(2)}, u32[]{:S(2)}) %collective-permute-start.3) | collective-permute-done | bytes 104480 | tf_op jit(solution)/shard_map/ppermute | solution.py:17
  39.5 0.2 copy.18
  39.6 47.2 %add_multiply_fusion = f32[32,128,1536]{2,1,0:T(8,128)} fusion(bf16[32,128,1536]{2,1,0:T(8,128)(2,1)} %param.6, bf16[34,128,1536]{2,1,0:T(8,128)(2,1)} %copy-done.1, bf16[34,1,1536]{2,1,0:T(2,128)(2,1)S(1)} %copy.18, bf16[34,1,1536]{2,1,0:T(2,128)(2,1)S(1)} %copy.16, bf16[1,128,1536]{2,1,0:T(8,128)(2,1)S(1)} %collective-permute-done.1, ...), kind=kLoop, calls=%fused_computation.1 | loop fusion | flops 264241152 | bytes 52113408 | tf_op jit(solution)/shard_map/div | solution.py:29
  86.8 0.0 copy-done
  86.9 18.7 %multiply_reduce_fusion.1 = (f32[4096]{0:T(1024)S(1)}, f32[4096,128]{0,1:T(8,128)S(1)}) fusion(f32[4096,1536]{1,0:T(8,128)} %bitcast.9, bf16[1536,128]{1,0:T(8,128)(2,1)S(1)} %copy-done), kind=kOutput, calls=%fused_computation.19 | convolution fusion | flops 9664720896 | bytes 27672576 | tf_op jit(solution)/shard_map/dot_general | solution.py:39
  105.6 0.0 copy-start.2
  105.6 0.0 copy-start.3
  105.6 1.9 copy.19
  107.5 2.6 gather_fusion
  110.1 0.8 broadcast_select_fusion
  111.0 0.0 all-reduce.2.cloned.1.call-update
  111.0 253.3 %all-reduce.2.cloned.1.call-done = f32[512,128]{1,0:T(8,128)} async-done(((f32[512,128]{1,0:T(8,128)}), f32[512,128]{1,0:T(8,128)}) %all-reduce.2.cloned.1.call-update) | async-done | bytes 262160 | tf_op jit(solution)/shard_map/psum | solution.py:41
  364.3 1.1 multiply_reduce_fusion.2
  365.4 9.2 %multiply_reduce_fusion = f32[4096]{0:T(1024)S(1)} fusion(f32[4096,128]{0,1:T(8,128)S(1)} %get-tuple-element.10, f32[512,128]{1,0:T(8,128)} %all-reduce.2.cloned.1.call-done, f32[512]{0:T(512)S(1)} %multiply_reduce_fusion.2, f32[4096]{0:T(1024)S(1)} %get-tuple-element.9), kind=kOutput, calls=%fused_computation.18 | convolution fusion | flops 3231707136 | bytes 2394112 | tf_op jit(solution)/shard_map/dot_general | solution.py:44
  374.6 0.0 copy-done.2
  374.6 0.0 copy-done.3
  374.7 0.6 fusion.4
  (5 shorter events, 0.1 us)
Async XLA Ops:
  6.5 80.3 %copy-start = (bf16[1536,128]{1,0:T(8,128)(2,1)S(1)}, bf16[1536,128]{1,0:T(8,128)(2,1)}, u32[]{:S(2)}) copy-start(bf16[1536,128]{1,0:T(8,128)(2,1)} %param.7) | copy-start | bytes 1179652
  6.5 357.8 %all-reduce.2.cloned.1.call-start = ((), (), s32[]{:S(2)}) async-start(), calls=%async_computation | async-start | bytes 524288 | tf_op jit(solution)/shard_map/psum | solution.py:41
  7.8 9.1 %collective-permute-start = (bf16[1,128,1536]{2,1,0:T(8,128)(2,1)S(1)}, bf16[1,128,1536]{2,1,0:T(8,128)(2,1)S(1)}, u32[]{:S(2)}, u32[]{:S(2)}) collective-permute-start(bf16[1,128,1536]{2,1,0:T(8,128)(2,1)S(1)} %get-tuple-element.8), channel_id=1, source_target_pairs={{0,32},{32,64},{64,96},{96,128},{128,160},{160,192},{192,224},{1,3... | collective-permute-start | bytes 1179656 | tf_op jit(solution)/shard_map/ppermute | solution.py:14
  9.7 13.9 %collective-permute-start.1 = (bf16[1,128,1536]{2,1,0:T(8,128)(2,1)S(1)}, bf16[1,128,1536]{2,1,0:T(8,128)(2,1)S(1)}, u32[]{:S(2)}, u32[]{:S(2)}) collective-permute-start(bf16[1,128,1536]{2,1,0:T(8,128)(2,1)S(1)} %get-tuple-element.7), channel_id=1, source_target_pairs={{32,0},{64,32},{96,64},{128,96},{160,128},{192,160},{224,192},{33,... | collective-permute-start | bytes 1179656 | tf_op jit(solution)/shard_map/ppermute | solution.py:17
  23.6 4.8 %copy-start.1 = (bf16[34,128,1536]{2,1,0:T(8,128)(2,1)}, bf16[34,128,1536]{2,1,0:T(8,128)(2,1)S(1)}, u32[]{:S(2)}) copy-start(bf16[34,128,1536]{2,1,0:T(8,128)(2,1)S(1)} %constant_dynamic-update-slice_fusion) | copy-start | bytes 40108036
  28.8 6.3 %collective-permute-start.2 = (bf16[34,1,1536]{2,0,1:T(8,128)(2,1)S(1)}, bf16[34,1,1536]{2,0,1:T(8,128)(2,1)S(1)}, u32[]{:S(2)}, u32[]{:S(2)}) collective-permute-start(bf16[34,1,1536]{2,0,1:T(8,128)(2,1)S(1)} %copy.15), channel_id=1, source_target_pairs={{0,1},{1,2},{2,3},{3,4},{4,5},{5,6},{6,7},{7,8},{8,9},{9,10},{10,1... | collective-permute-start | bytes 313352 | tf_op jit(solution)/shard_map/ppermute | solution.py:14
  32.7 6.8 %collective-permute-start.3 = (bf16[34,1,1536]{2,0,1:T(8,128)(2,1)S(1)}, bf16[34,1,1536]{2,0,1:T(8,128)(2,1)S(1)}, u32[]{:S(2)}, u32[]{:S(2)}) collective-permute-start(bf16[34,1,1536]{2,0,1:T(8,128)(2,1)S(1)} %copy.17), channel_id=1, source_target_pairs={{1,0},{2,1},{3,2},{4,3},{5,4},{6,5},{7,6},{8,7},{9,8},{10,9},{11,1... | collective-permute-start | bytes 313352 | tf_op jit(solution)/shard_map/ppermute | solution.py:17
  105.6 269.0 %copy-start.2 = (f32[32,128]{1,0:T(8,128)S(1)}, f32[32,128]{1,0:T(8,128)}, u32[]{:S(2)}) copy-start(f32[32,128]{1,0:T(8,128)} %param.8) | copy-start | bytes 49156
  105.6 269.0 %copy-start.3 = (s32[32,128]{1,0:T(8,128)S(1)}, s32[32,128]{1,0:T(8,128)}, u32[]{:S(2)}) copy-start(s32[32,128]{1,0:T(8,128)} %param.9) | copy-start | bytes 49156
Sparse Core Ops, SparseCore 0:
  111.1 253.1 all-reduce.1
where the time goes:
time: 382 us
  waiting for transfers between devices  261 us (68%)
  other arithmetic  51.2 us (13%)
  matrix products  27.9 us (7%)
  local copies, waits for them, and re-layouts  18 us (5%)
  between operations  13.6 us (4%)
  starting transfers between devices  10.7 us (3%)
    psum x1, waiting for transfers between devices, shards(): pick_rows = lax.psum(local_rows, ('rows', 'cols'))  253 us
    div x1, other arithmetic, window_sum(): return total / 9.0  47.2 us
    dot_general x1, matrix products, shards(): projected = jnp.dot(pooled, proj_full, precision=lax.Precision.HIGHEST)  18.7 us
    unnamed x10, local copies, waits for them, and re-layouts  11.6 us
    dot_general x1, matrix products, shards(): jnp.dot(projected, pick_rows.T, precision=lax.Precision.HIGHEST)  9.21 us
  transfers between devices with their start and end apart: 5, of which 4 were waited for; matrix products, arithmetic and copies ran while one was open for 2% of the time, Pallas kernels for 0%

commit v1 on v0

--- a/solution.py
+++ b/solution.py
@@ -38,7 +38,7 @@
     pooled = window_sum(padded, rows_dev, cols_dev).reshape(rows_dev * cols_dev, channels)
     projected = jnp.dot(pooled, proj_full, precision=lax.Precision.HIGHEST)
     local_rows = jnp.where(owned[:, None], projected[pick_slot], jnp.float32(0.0))
-    pick_rows = lax.psum(local_rows, ("rows", "cols"))
+    pick_rows = lax.psum(lax.psum(local_rows, "rows"), "cols")
     pick_sq = jnp.sum(pick_rows * pick_rows, axis=1)
     own_sq = jnp.sum(projected * projected, axis=1)
     inner_prod = jnp.dot(projected, pick_rows.T, precision=lax.Precision.HIGHEST)

time: 382 us -> 344 us (0.901)
  waiting for transfers between devices: 261 us -> 222 us
    psum x1 -> x2, waiting for transfers between devices: 253 us -> 215 us  [shards(): pick_rows = lax.psum(lax.psum(local_rows, 'rows'), 'cols')]
  transfers between devices with their start and end apart: 5 -> 6, of which waited for: 4 -> 5; matrix products, arithmetic and copies ran while one was open for 2% -> 2% of each run, Pallas kernels for 0% -> 0%
where the time goes in v1:
time: 344 us
  waiting for transfers between devices  222 us (65%)
  other arithmetic  51.2 us (15%)
  matrix products  27.8 us (8%)
  local copies, waits for them, and re-layouts  18 us (5%)
  between operations  13.6 us (4%)
  starting transfers between devices  10.9 us (3%)
    psum x2, waiting for transfers between devices, shards(): pick_rows = lax.psum(lax.psum(local_rows, 'rows'), 'cols')  215 us
    div x1, other arithmetic, window_sum(): return total / 9.0  47.2 us
    dot_general x1, matrix products, shards(): projected = jnp.dot(pooled, proj_full, precision=lax.Precision.HIGHEST)  18.7 us
    unnamed x10, local copies, waits for them, and re-layouts  11.6 us
    dot_general x1, matrix products, shards(): jnp.dot(projected, pick_rows.T, precision=lax.Precision.HIGHEST)  9.02 us
  transfers between devices with their start and end apart: 6, of which 5 were waited for; matrix products, arithmetic and copies ran while one was open for 2% of the time, Pallas kernels for 0%

profile of v1, /device:TPU:2, one launch (start us, length us, event | category | flops | bytes accessed | tf_op | source)
XLA Modules:
  0.0 343.7 jit_solution(8365192781819268430)
XLA Ops:
  6.5 0.0 copy-start
  6.5 0.0 all-reduce.3.cloned.1.call-start
  6.5 1.2 fusion.6
  7.8 1.9 collective-permute-start
  9.7 3.6 %collective-permute-start.1 = (bf16[1,128,1536]{2,1,0:T(8,128)(2,1)S(1)}, bf16[1,128,1536]{2,1,0:T(8,128)(2,1)S(1)}, u32[]{:S(2)}, u32[]{:S(2)}) collective-permute-start(bf16[1,128,1536]{2,1,0:T(8,128)(2,1)S(1)} %get-tuple-element.7), channel_id=1, source_target_pairs={{32,0},{64,32},{96,64},{128,96},{160,128},{192,160},{224,192},{33,... | collective-permute-start | bytes 1179656 | tf_op jit(solution)/shard_map/ppermute | solution.py:17
  13.3 0.7 broadcast_compare_fusion
  14.0 0.7 compare_select_fusion
  14.7 2.1 collective-permute-done
  16.9 6.7 %constant_dynamic-update-slice_fusion.1 = bf16[34,128,1536]{2,1,0:T(8,128)(2,1)S(1)} fusion(bf16[34,128,1536]{2,1,0:T(8,128)(2,1)S(1)} %constant_dynamic-update-slice_fusion.2, bf16[32,128,1536]{2,1,0:T(8,128)(2,1)} %param.6), kind=kLoop, calls=%fused_computation.25 | loop fusion | bytes 25165824
  23.6 0.0 collective-permute-done.1
  23.6 0.0 copy-start.1
  23.6 4.8 %copy-done.1 = bf16[34,128,1536]{2,1,0:T(8,128)(2,1)} copy-done((bf16[34,128,1536]{2,1,0:T(8,128)(2,1)}, bf16[34,128,1536]{2,1,0:T(8,128)(2,1)S(1)}, u32[]{:S(2)}) %copy-start.1) | copy-done | bytes 13369368
  28.5 0.3 fusion.5
  28.8 3.8 %collective-permute-start.2 = (bf16[34,1,1536]{2,0,1:T(8,128)(2,1)S(1)}, bf16[34,1,1536]{2,0,1:T(8,128)(2,1)S(1)}, u32[]{:S(2)}, u32[]{:S(2)}) collective-permute-start(bf16[34,1,1536]{2,0,1:T(8,128)(2,1)S(1)} %copy.15), channel_id=1, source_target_pairs={{0,1},{1,2},{2,3},{3,4},{4,5},{5,6},{6,7},{7,8},{8,9},{9,10},{10,1... | collective-permute-start | bytes 313352 | tf_op jit(solution)/shard_map/ppermute | solution.py:14
  32.7 1.3 collective-permute-start.3
  34.0 1.1 collective-permute-done.2
  35.1 0.2 copy.16
  35.2 4.2 %collective-permute-done.3 = bf16[34,1,1536]{2,0,1:T(8,128)(2,1)S(1)} collective-permute-done((bf16[34,1,1536]{2,0,1:T(8,128)(2,1)S(1)}, bf16[34,1,1536]{2,0,1:T(8,128)(2,1)S(1)}, u32[]{:S(2)}, u32[]{:S(2)}) %collective-permute-start.3) | collective-permute-done | bytes 104480 | tf_op jit(solution)/shard_map/ppermute | solution.py:17
  39.5 0.2 copy.18
  39.6 47.2 %add_multiply_fusion = f32[32,128,1536]{2,1,0:T(8,128)} fusion(bf16[32,128,1536]{2,1,0:T(8,128)(2,1)} %param.6, bf16[34,128,1536]{2,1,0:T(8,128)(2,1)} %copy-done.1, bf16[34,1,1536]{2,1,0:T(2,128)(2,1)S(1)} %copy.18, bf16[34,1,1536]{2,1,0:T(2,128)(2,1)S(1)} %copy.16, bf16[1,128,1536]{2,1,0:T(8,128)(2,1)S(1)} %collective-permute-done.1, ...), kind=kLoop, calls=%fused_computation.1 | loop fusion | flops 264241152 | bytes 52113408 | tf_op jit(solution)/shard_map/div | solution.py:29
  86.9 0.0 copy-done
  86.9 18.7 %multiply_reduce_fusion.1 = (f32[4096]{0:T(1024)S(1)}, f32[4096,128]{0,1:T(8,128)S(1)}) fusion(f32[4096,1536]{1,0:T(8,128)} %bitcast.9, bf16[1536,128]{1,0:T(8,128)(2,1)S(1)} %copy-done), kind=kOutput, calls=%fused_computation.19 | convolution fusion | flops 9664720896 | bytes 27672576 | tf_op jit(solution)/shard_map/dot_general | solution.py:39
  105.6 0.0 copy-start.2
  105.6 0.0 copy-start.3
  105.6 1.9 copy.19
  107.5 2.6 gather_fusion
  110.1 0.8 broadcast_select_fusion
  111.0 0.0 all-reduce.3.cloned.1.call-update
  111.0 0.2 all-reduce.5.cloned.1.call-start
  111.2 65.4 %all-reduce.3.cloned.1.call-done = f32[512,128]{1,0:T(8,128)} async-done(((f32[512,128]{1,0:T(8,128)}), f32[512,128]{1,0:T(8,128)}) %all-reduce.3.cloned.1.call-update) | async-done | bytes 262160 | tf_op jit(solution)/shard_map/psum | solution.py:41
  176.6 0.0 all-reduce.5.cloned.1.call-update
  176.7 149.4 %all-reduce.5.cloned.1.call-done = f32[512,128]{1,0:T(8,128)} async-done(((f32[512,128]{1,0:T(8,128)}), f32[512,128]{1,0:T(8,128)}) %all-reduce.5.cloned.1.call-update) | async-done | bytes 262160 | tf_op jit(solution)/shard_map/psum | solution.py:41
  326.1 1.1 multiply_reduce_fusion.2
  327.2 9.0 %multiply_reduce_fusion = f32[4096]{0:T(1024)S(1)} fusion(f32[4096,128]{0,1:T(8,128)S(1)} %get-tuple-element.10, f32[512,128]{1,0:T(8,128)} %all-reduce.5.cloned.1.call-done, f32[512]{0:T(512)S(1)} %multiply_reduce_fusion.2, f32[4096]{0:T(1024)S(1)} %get-tuple-element.9), kind=kOutput, calls=%fused_computation.18 | convolution fusion | flops 3231707136 | bytes 2394112 | tf_op jit(solution)/shard_map/dot_general | solution.py:44
  336.2 0.0 copy-done.2
  336.2 0.0 copy-done.3
  336.2 0.6 fusion.4
  (5 shorter events, 0.1 us)
Async XLA Ops:
  6.5 80.3 %copy-start = (bf16[1536,128]{1,0:T(8,128)(2,1)S(1)}, bf16[1536,128]{1,0:T(8,128)(2,1)}, u32[]{:S(2)}) copy-start(bf16[1536,128]{1,0:T(8,128)(2,1)} %param.7) | copy-start | bytes 1179652
  6.5 170.1 %all-reduce.3.cloned.1.call-start = ((), (), s32[]{:S(2)}) async-start(), calls=%async_computation | async-start | bytes 524288 | tf_op jit(solution)/shard_map/psum | solution.py:41
  7.8 9.1 %collective-permute-start = (bf16[1,128,1536]{2,1,0:T(8,128)(2,1)S(1)}, bf16[1,128,1536]{2,1,0:T(8,128)(2,1)S(1)}, u32[]{:S(2)}, u32[]{:S(2)}) collective-permute-start(bf16[1,128,1536]{2,1,0:T(8,128)(2,1)S(1)} %get-tuple-element.8), channel_id=1, source_target_pairs={{0,32},{32,64},{64,96},{96,128},{128,160},{160,192},{192,224},{1,3... | collective-permute-start | bytes 1179656 | tf_op jit(solution)/shard_map/ppermute | solution.py:14
  9.7 13.9 %collective-permute-start.1 = (bf16[1,128,1536]{2,1,0:T(8,128)(2,1)S(1)}, bf16[1,128,1536]{2,1,0:T(8,128)(2,1)S(1)}, u32[]{:S(2)}, u32[]{:S(2)}) collective-permute-start(bf16[1,128,1536]{2,1,0:T(8,128)(2,1)S(1)} %get-tuple-element.7), channel_id=1, source_target_pairs={{32,0},{64,32},{96,64},{128,96},{160,128},{192,160},{224,192},{33,... | collective-permute-start | bytes 1179656 | tf_op jit(solution)/shard_map/ppermute | solution.py:17
  23.6 4.8 %copy-start.1 = (bf16[34,128,1536]{2,1,0:T(8,128)(2,1)}, bf16[34,128,1536]{2,1,0:T(8,128)(2,1)S(1)}, u32[]{:S(2)}) copy-start(bf16[34,128,1536]{2,1,0:T(8,128)(2,1)S(1)} %constant_dynamic-update-slice_fusion) | copy-start | bytes 40108036
  28.8 6.3 %collective-permute-start.2 = (bf16[34,1,1536]{2,0,1:T(8,128)(2,1)S(1)}, bf16[34,1,1536]{2,0,1:T(8,128)(2,1)S(1)}, u32[]{:S(2)}, u32[]{:S(2)}) collective-permute-start(bf16[34,1,1536]{2,0,1:T(8,128)(2,1)S(1)} %copy.15), channel_id=1, source_target_pairs={{0,1},{1,2},{2,3},{3,4},{4,5},{5,6},{6,7},{7,8},{8,9},{9,10},{10,1... | collective-permute-start | bytes 313352 | tf_op jit(solution)/shard_map/ppermute | solution.py:14
  32.7 6.8 %collective-permute-start.3 = (bf16[34,1,1536]{2,0,1:T(8,128)(2,1)S(1)}, bf16[34,1,1536]{2,0,1:T(8,128)(2,1)S(1)}, u32[]{:S(2)}, u32[]{:S(2)}) collective-permute-start(bf16[34,1,1536]{2,0,1:T(8,128)(2,1)S(1)} %copy.17), channel_id=1, source_target_pairs={{1,0},{2,1},{3,2},{4,3},{5,4},{6,5},{7,6},{8,7},{9,8},{10,9},{11,1... | collective-permute-start | bytes 313352 | tf_op jit(solution)/shard_map/ppermute | solution.py:17
  105.6 230.6 %copy-start.2 = (f32[32,128]{1,0:T(8,128)S(1)}, f32[32,128]{1,0:T(8,128)}, u32[]{:S(2)}) copy-start(f32[32,128]{1,0:T(8,128)} %param.8) | copy-start | bytes 49156
  105.6 230.6 %copy-start.3 = (s32[32,128]{1,0:T(8,128)S(1)}, s32[32,128]{1,0:T(8,128)}, u32[]{:S(2)}) copy-start(s32[32,128]{1,0:T(8,128)} %param.9) | copy-start | bytes 49156
  111.0 215.1 %all-reduce.5.cloned.1.call-start = ((), (), s32[]{:S(2)}) async-start(), calls=%async_computation.1 | async-start | bytes 524288 | tf_op jit(solution)/shard_map/psum | solution.py:41
Sparse Core Ops, SparseCore 0:
  111.1 65.4 all-reduce.2
  180.5 145.5 all-reduce.4
